TPU v7x, 256 devices: a whole 4x4x8 slice. The times are simulated.
256 devices in a mesh: op: 32 (over z_lo, x, core), term: 8 (over z_hi, y).
Axes of the slice: x: 4, y: 4, z: 8 (z_hi: 2, z_lo: 4; z = z_hi * 4 + z_lo), core: 2. Of those that a mesh axis runs over, the one named last changes fastest.
Arguments:
- wavefunction: float32 [32, 384, 384], P('op'), may hold values from -6 to 6
- left_dims: int32 [32], P('op'), may hold values from 192 to 384
- right_dims: int32 [32], P('op'), may hold values from 192 to 384
- left_operators: float32 [32, 8, 384, 384], P('op', 'term'), may hold values from -0.109375 to 0.109375
- right_operators: float32 [32, 8, 384, 384], P('op', 'term'), may hold values from -0.3125 to 0.3125
- charges: int32 [32, 8], P('op', 'term'), may hold values from 0 to 11
Outputs:
- applied: float32 [32, 384, 384], P('op', 'term')
Inputs may be any that keep to these rules, and one draw needn't show every extreme that they name: `charges`: a term of source sector s acts into sector (s + charge) mod 32.
All inputs are finite; a program needn't handle non-finite values.
Results may differ from a plain program's by a relative error of at most 0.0003.
Values sent between devices are 32-bit elements; how exact they have to be, the bound alone decides.
A program may use at most 64 MiB of HBM per device.

v0:
```python
import jax
import jax.numpy as jnp
from jax import lax
from jax.sharding import PartitionSpec as P

CHARGES = 12


TOP_CHARGE = lax.Precision.HIGHEST


def shifted(value, axis, steps):
    count = lax.axis_size(axis)
    pairs = [(source, (source + steps) % count) for source in range(count)]
    return lax.ppermute(value, axis, pairs)


def cut_along(array, dim, peers):
    before, after = (array.shape[:dim], array.shape[dim + 1 :])
    return jnp.moveaxis(array.reshape(*before, peers, -1, *after), dim, 0)


def summed_on_arrival(array, axis, dim):
    pieces = cut_along(array, dim, lax.axis_size(axis))
    arrived = lax.all_to_all(pieces, axis, split_axis=0, concat_axis=0, tiled=True)
    return arrived.sum(axis=0)


def on_device(wavefunction, left_dims, right_dims, left_operators, right_operators, charges):
    block_order = wavefunction.shape[1]
    positions = jnp.arange(block_order)
    mask_applied = wavefunction[0] * (
        (positions[:, None] < left_dims[0]) & (positions[None, :] < right_dims[0])
    ).astype(jnp.float32)
    left_product = jnp.einsum("ims,sd->imd", left_operators[0], mask_applied, precision=TOP_CHARGE)
    term_contribution = jnp.einsum(
        "opu,oru->opr", left_product, right_operators[0], precision=TOP_CHARGE
    )
    term_charge = charges[0]

    def charge_part(charge_value):
        selector = (term_charge == charge_value).astype(jnp.float32)
        return jnp.einsum("t,tab->ab", selector, term_contribution, precision=TOP_CHARGE)

    def advance_full(cycle_step, carried):
        carried = shifted(carried, "op", 1)
        return carried + charge_part(CHARGES - 1 - cycle_step)

    summed = lax.fori_loop(1, CHARGES, advance_full, charge_part(CHARGES - 1))
    owned = summed_on_arrival(summed, "term", 0)
    row_count = owned.shape[0]
    row_index = lax.axis_index("term") * row_count + jnp.arange(row_count)
    live_rows = ((row_index[:, None] < left_dims[0]) & (positions[None, :] < right_dims[0])).astype(
        jnp.float32
    )
    return (owned * live_rows)[None]


def solution(mesh):
    in_specs = (
        P("op", None, None),
        P("op"),
        P("op"),
        P("op", "term", None, None),
        P("op", "term", None, None),
        P("op", "term"),
    )
    out_specs = P("op", "term", None)
    return jax.shard_map(
        on_device, mesh=mesh, in_specs=in_specs, out_specs=out_specs, check_vma=False
    )
```

profile of v0, /device:TPU:0, one launch (start us, length us, event | category | flops | bytes accessed | tf_op | source)
XLA Modules:
  0.0 192.4 jit_solution(1957331014433174206)
XLA Ops:
  0.0 0.0 copy-start
  2.0 3.4 %fusion.2 = f32[384,384]{1,0:T(8,128)S(1)} fusion(f32[1,1,384,384]{3,2,1,0:T(8,128)} %param.11, f32[1,384,384]{2,1,0:T(8,128)} %param.8, pred[384]{0:T(512)(128)(4,1)S(1)} %get-tuple-element.96, pred[384]{0:T(512)(128)(4,1)S(1)} %get-tuple-element.95), kind=kOutput, calls=%fused_computation.3 | convolution fusion | flops 679772160 | bytes 1770240 | tf_op jit(solution)/shard_map/ims,sd->imd/dot_general | solution.py:35
  5.4 0.0 copy-done
  5.4 2.9 %broadcast_multiply_fusion = (f32[384,384]{1,0:T(8,128)}, f32[384,384]{1,0:T(8,128)S(1)}) fusion(f32[]{:T(128)} %bitcast.6, f32[384,384]{1,0:T(8,128)S(1)} %fusion.2, f32[1,1,384,384]{3,2,1,0:T(8,128)S(1)} %copy-done), kind=kOutput, calls=%fused_computation.9 | convolution fusion | flops 679624704 | bytes 2359300 | tf_op jit(solution)/shard_map/opu,oru->opr/dot_general | solution.py:36
  8.3 160.8 %while.13 = (s32[]{:T(128)}, f32[384,384]{1,0:T(8,128)}, s32[1]{0:T(128)}, f32[1,384,384]{2,1,0:T(8,128)S(1)}, s32[]{:T(128)}, /*index=5*/s32[]{:T(128)}) while((s32[]{:T(128)}, f32[384,384]{1,0:T(8,128)}, s32[1]{0:T(128)}, f32[1,384,384]{2,1,0:T(8,128)S(1)}, s32[]{:T(128)}, /*index=5*/s32[]{:T(128)}) %tuple.33), condition=%wide.region_1.0_spmd, body=%wide.region_0.0_spmd.sunk | while | flops 294917 | bytes 4128907 | solution.py:49
  8.3 0.0 collective-permute-start
  8.9 12.8 %collective-permute-done = f32[384,384]{1,0:T(8,128)S(1)} collective-permute-done((f32[384,384]{1,0:T(8,128)}, f32[384,384]{1,0:T(8,128)S(1)}, u32[]{:S(2)}, u32[]{:S(2)}) %collective-permute-start) | collective-permute-done | bytes 589856 | tf_op jit(solution)/shard_map/while/body/eval_jaxpr/ppermute | solution.py:15
  21.7 0.9 bitcast_add_fusion.2
  22.6 0.0 collective-permute-start
  23.3 12.8 %collective-permute-done = f32[384,384]{1,0:T(8,128)S(1)} collective-permute-done((f32[384,384]{1,0:T(8,128)}, f32[384,384]{1,0:T(8,128)S(1)}, u32[]{:S(2)}, u32[]{:S(2)}) %collective-permute-start) | collective-permute-done | bytes 589856 | tf_op jit(solution)/shard_map/while/body/eval_jaxpr/ppermute | solution.py:15
  36.0 0.9 bitcast_add_fusion.2
  36.9 0.0 collective-permute-start
  37.6 12.8 %collective-permute-done = f32[384,384]{1,0:T(8,128)S(1)} collective-permute-done((f32[384,384]{1,0:T(8,128)}, f32[384,384]{1,0:T(8,128)S(1)}, u32[]{:S(2)}, u32[]{:S(2)}) %collective-permute-start) | collective-permute-done | bytes 589856 | tf_op jit(solution)/shard_map/while/body/eval_jaxpr/ppermute | solution.py:15
  50.3 0.9 bitcast_add_fusion.2
  51.2 0.0 collective-permute-start
  51.9 12.8 %collective-permute-done = f32[384,384]{1,0:T(8,128)S(1)} collective-permute-done((f32[384,384]{1,0:T(8,128)}, f32[384,384]{1,0:T(8,128)S(1)}, u32[]{:S(2)}, u32[]{:S(2)}) %collective-permute-start) | collective-permute-done | bytes 589856 | tf_op jit(solution)/shard_map/while/body/eval_jaxpr/ppermute | solution.py:15
  64.7 0.9 bitcast_add_fusion.2
  65.5 0.0 collective-permute-start
  66.2 12.8 %collective-permute-done = f32[384,384]{1,0:T(8,128)S(1)} collective-permute-done((f32[384,384]{1,0:T(8,128)}, f32[384,384]{1,0:T(8,128)S(1)}, u32[]{:S(2)}, u32[]{:S(2)}) %collective-permute-start) | collective-permute-done | bytes 589856 | tf_op jit(solution)/shard_map/while/body/eval_jaxpr/ppermute | solution.py:15
  79.0 0.9 bitcast_add_fusion.2
  79.9 0.0 collective-permute-start
  80.5 12.8 %collective-permute-done = f32[384,384]{1,0:T(8,128)S(1)} collective-permute-done((f32[384,384]{1,0:T(8,128)}, f32[384,384]{1,0:T(8,128)S(1)}, u32[]{:S(2)}, u32[]{:S(2)}) %collective-permute-start) | collective-permute-done | bytes 589856 | tf_op jit(solution)/shard_map/while/body/eval_jaxpr/ppermute | solution.py:15
  93.3 0.9 bitcast_add_fusion.2
  94.2 0.0 collective-permute-start
  94.8 12.8 %collective-permute-done = f32[384,384]{1,0:T(8,128)S(1)} collective-permute-done((f32[384,384]{1,0:T(8,128)}, f32[384,384]{1,0:T(8,128)S(1)}, u32[]{:S(2)}, u32[]{:S(2)}) %collective-permute-start) | collective-permute-done | bytes 589856 | tf_op jit(solution)/shard_map/while/body/eval_jaxpr/ppermute | solution.py:15
  107.6 0.9 bitcast_add_fusion.2
  108.5 0.0 collective-permute-start
  109.2 12.8 %collective-permute-done = f32[384,384]{1,0:T(8,128)S(1)} collective-permute-done((f32[384,384]{1,0:T(8,128)}, f32[384,384]{1,0:T(8,128)S(1)}, u32[]{:S(2)}, u32[]{:S(2)}) %collective-permute-start) | collective-permute-done | bytes 589856 | tf_op jit(solution)/shard_map/while/body/eval_jaxpr/ppermute | solution.py:15
  121.9 0.9 bitcast_add_fusion.2
  122.8 0.0 collective-permute-start
  123.5 12.8 %collective-permute-done = f32[384,384]{1,0:T(8,128)S(1)} collective-permute-done((f32[384,384]{1,0:T(8,128)}, f32[384,384]{1,0:T(8,128)S(1)}, u32[]{:S(2)}, u32[]{:S(2)}) %collective-permute-start) | collective-permute-done | bytes 589856 | tf_op jit(solution)/shard_map/while/body/eval_jaxpr/ppermute | solution.py:15
  136.2 0.9 bitcast_add_fusion.2
  137.1 0.0 collective-permute-start
  137.8 12.9 %collective-permute-done = f32[384,384]{1,0:T(8,128)S(1)} collective-permute-done((f32[384,384]{1,0:T(8,128)}, f32[384,384]{1,0:T(8,128)S(1)}, u32[]{:S(2)}, u32[]{:S(2)}) %collective-permute-start) | collective-permute-done | bytes 589856 | tf_op jit(solution)/shard_map/while/body/eval_jaxpr/ppermute | solution.py:15
  150.6 0.9 bitcast_add_fusion.2
  151.5 0.0 collective-permute-start
  152.2 16.1 %collective-permute-done = f32[384,384]{1,0:T(8,128)S(1)} collective-permute-done((f32[384,384]{1,0:T(8,128)}, f32[384,384]{1,0:T(8,128)S(1)}, u32[]{:S(2)}, u32[]{:S(2)}) %collective-permute-start) | collective-permute-done | bytes 589856 | tf_op jit(solution)/shard_map/while/body/eval_jaxpr/ppermute | solution.py:15
  168.2 0.9 bitcast_add_fusion.2
  169.1 10.0 %all-to-all-start = ((f32[8,48,384]{2,1,0:T(8,128)}), f32[8,48,384]{2,1,0:T(8,128)S(1)}, u32[]{:S(2)}, u32[]{:S(2)}) async-start(f32[8,48,384]{2,1,0:T(8,128)} %bitcast.11), calls=%async_computation | async-start | bytes 1179648 | tf_op jit(solution)/shard_map/all_to_all | solution.py:25
  179.2 12.4 %all-to-all-done = f32[8,48,384]{2,1,0:T(8,128)S(1)} async-done(((f32[8,48,384]{2,1,0:T(8,128)}), f32[8,48,384]{2,1,0:T(8,128)S(1)}, u32[]{:S(2)}, u32[]{:S(2)}) %all-to-all-start) | async-done | bytes 589856 | tf_op jit(solution)/shard_map/all_to_all | solution.py:25
  191.7 0.7 bitcast_select_fusion
  (3 shorter events, 0.0 us)
Async XLA Ops:
  0.0 5.4 %copy-start = (f32[1,1,384,384]{3,2,1,0:T(8,128)S(1)}, f32[1,1,384,384]{3,2,1,0:T(8,128)}, u32[]{:S(2)}) copy-start(f32[1,1,384,384]{3,2,1,0:T(8,128)} %param.12) | copy-start | bytes 1769476
  8.3 13.4 %collective-permute-start = (f32[384,384]{1,0:T(8,128)}, f32[384,384]{1,0:T(8,128)S(1)}, u32[]{:S(2)}, u32[]{:S(2)}) collective-permute-start(f32[384,384]{1,0:T(8,128)} %get-tuple-element.129), channel_id=1, source_target_pairs={{0,8},{8,16},{16,24},{24,32},{32,40},{40,48},{48,56},{56,64},{64,7... | collective-permute-start | bytes 1769480 | tf_op jit(solution)/shard_map/while/body/eval_jaxpr/ppermute | solution.py:15
  22.6 13.4 %collective-permute-start = (f32[384,384]{1,0:T(8,128)}, f32[384,384]{1,0:T(8,128)S(1)}, u32[]{:S(2)}, u32[]{:S(2)}) collective-permute-start(f32[384,384]{1,0:T(8,128)} %get-tuple-element.129), channel_id=1, source_target_pairs={{0,8},{8,16},{16,24},{24,32},{32,40},{40,48},{48,56},{56,64},{64,7... | collective-permute-start | bytes 1769480 | tf_op jit(solution)/shard_map/while/body/eval_jaxpr/ppermute | solution.py:15
  36.9 13.4 %collective-permute-start = (f32[384,384]{1,0:T(8,128)}, f32[384,384]{1,0:T(8,128)S(1)}, u32[]{:S(2)}, u32[]{:S(2)}) collective-permute-start(f32[384,384]{1,0:T(8,128)} %get-tuple-element.129), channel_id=1, source_target_pairs={{0,8},{8,16},{16,24},{24,32},{32,40},{40,48},{48,56},{56,64},{64,7... | collective-permute-start | bytes 1769480 | tf_op jit(solution)/shard_map/while/body/eval_jaxpr/ppermute | solution.py:15
  51.2 13.4 %collective-permute-start = (f32[384,384]{1,0:T(8,128)}, f32[384,384]{1,0:T(8,128)S(1)}, u32[]{:S(2)}, u32[]{:S(2)}) collective-permute-start(f32[384,384]{1,0:T(8,128)} %get-tuple-element.129), channel_id=1, source_target_pairs={{0,8},{8,16},{16,24},{24,32},{32,40},{40,48},{48,56},{56,64},{64,7... | collective-permute-start | bytes 1769480 | tf_op jit(solution)/shard_map/while/body/eval_jaxpr/ppermute | solution.py:15
  65.5 13.4 %collective-permute-start = (f32[384,384]{1,0:T(8,128)}, f32[384,384]{1,0:T(8,128)S(1)}, u32[]{:S(2)}, u32[]{:S(2)}) collective-permute-start(f32[384,384]{1,0:T(8,128)} %get-tuple-element.129), channel_id=1, source_target_pairs={{0,8},{8,16},{16,24},{24,32},{32,40},{40,48},{48,56},{56,64},{64,7... | collective-permute-start | bytes 1769480 | tf_op jit(solution)/shard_map/while/body/eval_jaxpr/ppermute | solution.py:15
  79.9 13.4 %collective-permute-start = (f32[384,384]{1,0:T(8,128)}, f32[384,384]{1,0:T(8,128)S(1)}, u32[]{:S(2)}, u32[]{:S(2)}) collective-permute-start(f32[384,384]{1,0:T(8,128)} %get-tuple-element.129), channel_id=1, source_target_pairs={{0,8},{8,16},{16,24},{24,32},{32,40},{40,48},{48,56},{56,64},{64,7... | collective-permute-start | bytes 1769480 | tf_op jit(solution)/shard_map/while/body/eval_jaxpr/ppermute | solution.py:15
  94.2 13.4 %collective-permute-start = (f32[384,384]{1,0:T(8,128)}, f32[384,384]{1,0:T(8,128)S(1)}, u32[]{:S(2)}, u32[]{:S(2)}) collective-permute-start(f32[384,384]{1,0:T(8,128)} %get-tuple-element.129), channel_id=1, source_target_pairs={{0,8},{8,16},{16,24},{24,32},{32,40},{40,48},{48,56},{56,64},{64,7... | collective-permute-start | bytes 1769480 | tf_op jit(solution)/shard_map/while/body/eval_jaxpr/ppermute | solution.py:15
  108.5 13.4 %collective-permute-start = (f32[384,384]{1,0:T(8,128)}, f32[384,384]{1,0:T(8,128)S(1)}, u32[]{:S(2)}, u32[]{:S(2)}) collective-permute-start(f32[384,384]{1,0:T(8,128)} %get-tuple-element.129), channel_id=1, source_target_pairs={{0,8},{8,16},{16,24},{24,32},{32,40},{40,48},{48,56},{56,64},{64,7... | collective-permute-start | bytes 1769480 | tf_op jit(solution)/shard_map/while/body/eval_jaxpr/ppermute | solution.py:15
  122.8 13.4 %collective-permute-start = (f32[384,384]{1,0:T(8,128)}, f32[384,384]{1,0:T(8,128)S(1)}, u32[]{:S(2)}, u32[]{:S(2)}) collective-permute-start(f32[384,384]{1,0:T(8,128)} %get-tuple-element.129), channel_id=1, source_target_pairs={{0,8},{8,16},{16,24},{24,32},{32,40},{40,48},{48,56},{56,64},{64,7... | collective-permute-start | bytes 1769480 | tf_op jit(solution)/shard_map/while/body/eval_jaxpr/ppermute | solution.py:15
  137.1 13.5 %collective-permute-start = (f32[384,384]{1,0:T(8,128)}, f32[384,384]{1,0:T(8,128)S(1)}, u32[]{:S(2)}, u32[]{:S(2)}) collective-permute-start(f32[384,384]{1,0:T(8,128)} %get-tuple-element.129), channel_id=1, source_target_pairs={{0,8},{8,16},{16,24},{24,32},{32,40},{40,48},{48,56},{56,64},{64,7... | collective-permute-start | bytes 1769480 | tf_op jit(solution)/shard_map/while/body/eval_jaxpr/ppermute | solution.py:15
  151.5 16.7 %collective-permute-start = (f32[384,384]{1,0:T(8,128)}, f32[384,384]{1,0:T(8,128)S(1)}, u32[]{:S(2)}, u32[]{:S(2)}) collective-permute-start(f32[384,384]{1,0:T(8,128)} %get-tuple-element.129), channel_id=1, source_target_pairs={{0,8},{8,16},{16,24},{24,32},{32,40},{40,48},{48,56},{56,64},{64,7... | collective-permute-start | bytes 1769480 | tf_op jit(solution)/shard_map/while/body/eval_jaxpr/ppermute | solution.py:15
  169.1 22.5 %all-to-all-start = ((f32[8,48,384]{2,1,0:T(8,128)}), f32[8,48,384]{2,1,0:T(8,128)S(1)}, u32[]{:S(2)}, u32[]{:S(2)}) async-start(f32[8,48,384]{2,1,0:T(8,128)} %bitcast.11), calls=%async_computation | async-start | bytes 1179648 | tf_op jit(solution)/shard_map/all_to_all | solution.py:25
where the time goes:
time: 193 us; the launch traced here: 192 us
  waiting for transfers between devices  156 us (81%)
  other arithmetic  10.5 us (5%)
  starting transfers between devices  10.1 us (5%)
  loops' own time  7.21 us (4%)
  matrix products  6.25 us (3%)
  between operations  2.03 us (1%)
    ppermute x11, waiting for transfers between devices, shifted(): return lax.ppermute(value, axis, pairs)  144 us
    all_to_all x1, waiting for transfers between devices, summed_on_arrival(): lax.all_to_all(pieces, axis, split_axis=0, concat_axis=0, tiled=True)  12.4 us
    all_to_all x1, starting transfers between devices, summed_on_arrival(): lax.all_to_all(pieces, axis, split_axis=0, concat_axis=0, tiled=True)  10 us
    add x11, other arithmetic, advance_full(): return carried + charge_part(CHARGES - 1 - cycle_step)  9.76 us
    another operation x1, loops' own time, on_device(): summed = lax.fori_loop(1, CHARGES, advance_full, charge_part(CHARGES - 1))  7.21 us
  transfers between devices with their start and end apart: 12, of which 12 were waited for; matrix products, arithmetic and copies ran while one was open for 0% of the time, Pallas kernels for 0%

commit v1 on v0

v1 whole, which is shorter than its diff:
```python
import jax
import jax.numpy as jnp
from jax import lax
from jax.sharding import PartitionSpec as P

CHARGES = 12
TOP_CHARGE = lax.Precision.HIGHEST


def shifted(value, axis, steps):
    count = lax.axis_size(axis)
    pairs = [(source, (source + steps) % count) for source in range(count)]
    return lax.ppermute(value, axis, pairs)


def on_device(wavefunction, left_dims, right_dims, left_operators, right_operators, charges):
    block_order = wavefunction.shape[1]
    positions = jnp.arange(block_order)
    peers = lax.axis_size("term")
    rows = block_order // peers
    mask_applied = wavefunction[0] * (
        (positions[:, None] < left_dims[0]) & (positions[None, :] < right_dims[0])
    ).astype(jnp.float32)
    left_product = jnp.einsum("ims,sd->imd", left_operators[0], mask_applied, precision=TOP_CHARGE)
    contribution = jnp.einsum(
        "opu,oru->opr", left_product, right_operators[0], precision=TOP_CHARGE
    )[0]
    tag = jnp.broadcast_to(charges.astype(jnp.float32)[:, :, None], (peers, 8, block_order))
    pieces = jnp.concatenate([contribution.reshape(peers, rows, block_order), tag], axis=1)
    arrived = lax.all_to_all(pieces, "term", split_axis=0, concat_axis=0, tiled=True)
    blocks, tags = arrived[:, :rows], arrived[:, rows, 0]

    def charge_part(charge_value):
        chosen = (tags == charge_value)[:, None, None]
        return jnp.where(chosen, blocks, 0.0).sum(axis=0)

    summed = charge_part(CHARGES - 1)
    for charge_value in range(CHARGES - 2, -1, -1):
        summed = shifted(summed, "op", 1) + charge_part(charge_value)
    row_index = lax.axis_index("term") * rows + jnp.arange(rows)
    live_rows = ((row_index[:, None] < left_dims[0]) & (positions[None, :] < right_dims[0])).astype(
        jnp.float32
    )
    return (summed * live_rows)[None]


def solution(mesh):
    in_specs = (
        P("op", None, None),
        P("op"),
        P("op"),
        P("op", "term", None, None),
        P("op", "term", None, None),
        P("op", "term"),
    )
    out_specs = P("op", "term", None)
    return jax.shard_map(
        on_device, mesh=mesh, in_specs=in_specs, out_specs=out_specs, check_vma=False
    )
```

time: 193 us -> 124 us (0.64)
  waiting for transfers between devices: 156 us -> 84.4 us
  blocking collectives: 0 us -> 29.3 us
  starting transfers between devices: 10.1 us -> 0.91 us
  loops' own time: 7.21 us -> 0 us
  other arithmetic: 10.5 us -> 3.63 us
  matrix products: 6.25 us -> 3.81 us
    ppermute x11, waiting for transfers between devices: 144 us -> 84.4 us  [shifted(): return lax.ppermute(value, axis, pairs)]
    all_to_all x0 -> x1, blocking collectives: none -> 29.3 us  [on_device(): lax.all_to_all(pieces, 'term', split_axis=0, concat_axis=0, tiled=True)]
    all_to_all x1 -> x0, waiting for transfers between devices: 12.4 us -> none  [summed_on_arrival(): lax.all_to_all(pieces, axis, split_axis=0, concat_axis=0, tiled=True)]
    all_to_all x1 -> x0, starting transfers between devices: 10 us -> none  [summed_on_arrival(): lax.all_to_all(pieces, axis, split_axis=0, concat_axis=0, tiled=True)]
    add x11 -> x10, other arithmetic: 9.76 us -> 0.11 us  [on_device(): summed = shifted(summed, 'op', 1) + charge_part(charge_value)]
    another operation x1 -> x0, loops' own time: 7.21 us -> none  [on_device(): summed = lax.fori_loop(1, CHARGES, advance_full, charge_part(CHARGES - 1))]
  transfers between devices with their start and end apart: 12 -> 11, of which waited for: 12 -> 11; matrix products, arithmetic and copies ran while one was open for 0% -> 0% of each run, Pallas kernels for 0% -> 0%
where the time goes in v1:
time: 124 us
  waiting for transfers between devices  84.4 us (68%)
  blocking collectives  29.3 us (24%)
  matrix products  3.81 us (3%)
  other arithmetic  3.63 us (3%)
  between operations  2.2 us (2%)
    ppermute x11, waiting for transfers between devices, shifted(): return lax.ppermute(value, axis, pairs)  84.4 us
    all_to_all x1, blocking collectives, on_device(): lax.all_to_all(pieces, 'term', split_axis=0, concat_axis=0, tiled=True)  29.3 us
    dot_general x1, matrix products, on_device(): jnp.einsum('ims,sd->imd', left_operators[0], mask_applied, precision=TOP_...  2.54 us
  transfers between devices with their start and end apart: 11, of which 11 were waited for; matrix products, arithmetic and copies ran while one was open for 0% of the time, Pallas kernels for 0%

profile of v1, /device:TPU:0, one launch (start us, length us, event | category | flops | bytes accessed | tf_op | source)
XLA Modules:
  0.0 124.3 jit_solution(15501260117919431591)
XLA Ops:
  0.0 0.0 copy-start
  2.0 0.0 copy-done
  2.0 0.0 copy-start.1
  2.0 2.5 %fusion.2 = f32[384,384]{0,1:T(8,128)S(1)} fusion(f32[1,1,384,384]{3,2,1,0:T(8,128)S(1)} %copy-done, f32[1,384,384]{2,1,0:T(8,128)} %param.6, pred[384]{0:T(512)(128)(4,1)S(1)} %get-tuple-element.33, pred[384]{0:T(512)(128)(4,1)S(1)} %get-tuple-element.32), kind=kOutput, calls=%fused_computation.2 | convolution fusion | flops 679772160 | bytes 1770240 | tf_op jit(solution)/shard_map/ims,sd->imd/dot_general | solution.py:24
  4.6 0.0 copy-done.1
  4.6 1.3 %fusion = f32[8,48,384]{2,1,0:T(8,128)S(1)} fusion(f32[8,48,384]{2,1,0:T(8,128)S(1)} %bitcast.23, f32[1,1,384,384]{3,2,1,0:T(8,128)S(1)} %copy-done.1), kind=kOutput, calls=%fused_computation | convolution fusion | flops 679477248 | bytes 1769472 | tf_op jit(solution)/shard_map/opu,oru->opr/dot_general | solution.py:25
  5.9 0.1 concatenate.3
  5.9 29.3 %all_to_all.5 = f32[8,56,384]{2,1,0:T(8,128)S(1)} all-to-all(f32[8,56,384]{2,1,0:T(8,128)S(1)} %concatenate.3), channel_id=1, replica_groups=mesh['op'=32,'term'=8] {'term'}, dimensions={0} | all-to-all | bytes 1376256 | tf_op jit(solution)/shard_map/all_to_all | solution.py:30
  35.2 1.8 %compare_reduce_fusion = (pred[8]{0:T(512)(128)(4,1)S(1)}, pred[8]{0:T(512)(128)(4,1)S(1)}, pred[8]{0:T(512)(128)(4,1)S(1)}, pred[8]{0:T(512)(128)(4,1)S(1)}, pr...) fusion(f32[8,56,384]{2,1,0:T(8,128)S(1)} %all_to_all.5), kind=kLoop, calls=%fused_computation.23 | loop fusion | flops 96 | bytes 128 | tf_op jit(solution)/shard_map/eq | solution.py:34
  37.1 1.0 select_reduce_fusion
  38.1 0.1 collective-permute-start
  38.1 7.7 %collective-permute-done = f32[48,384]{1,0:T(8,128)S(1)} collective-permute-done((f32[48,384]{1,0:T(8,128)S(1)}, f32[48,384]{1,0:T(8,128)S(1)}, u32[]{:S(2)}, u32[]{:S(2)}) %collective-permute-start) | collective-permute-done | bytes 73760 | tf_op jit(solution)/shard_map/ppermute | solution.py:13
  45.8 0.1 collective-permute-start.1
  45.9 7.7 %collective-permute-done.1 = f32[48,384]{1,0:T(8,128)S(1)} collective-permute-done((f32[48,384]{1,0:T(8,128)S(1)}, f32[48,384]{1,0:T(8,128)S(1)}, u32[]{:S(2)}, u32[]{:S(2)}) %collective-permute-start.1) | collective-permute-done | bytes 73760 | tf_op jit(solution)/shard_map/ppermute | solution.py:13
  53.6 0.1 collective-permute-start.2
  53.7 7.7 %collective-permute-done.2 = f32[48,384]{1,0:T(8,128)S(1)} collective-permute-done((f32[48,384]{1,0:T(8,128)S(1)}, f32[48,384]{1,0:T(8,128)S(1)}, u32[]{:S(2)}, u32[]{:S(2)}) %collective-permute-start.2) | collective-permute-done | bytes 73760 | tf_op jit(solution)/shard_map/ppermute | solution.py:13
  61.4 0.1 collective-permute-start.3
  61.5 7.7 %collective-permute-done.3 = f32[48,384]{1,0:T(8,128)S(1)} collective-permute-done((f32[48,384]{1,0:T(8,128)S(1)}, f32[48,384]{1,0:T(8,128)S(1)}, u32[]{:S(2)}, u32[]{:S(2)}) %collective-permute-start.3) | collective-permute-done | bytes 73760 | tf_op jit(solution)/shard_map/ppermute | solution.py:13
  69.2 0.1 collective-permute-start.4
  69.2 7.7 %collective-permute-done.4 = f32[48,384]{1,0:T(8,128)S(1)} collective-permute-done((f32[48,384]{1,0:T(8,128)S(1)}, f32[48,384]{1,0:T(8,128)S(1)}, u32[]{:S(2)}, u32[]{:S(2)}) %collective-permute-start.4) | collective-permute-done | bytes 73760 | tf_op jit(solution)/shard_map/ppermute | solution.py:13
  76.9 0.1 collective-permute-start.5
  77.0 7.7 %collective-permute-done.5 = f32[48,384]{1,0:T(8,128)S(1)} collective-permute-done((f32[48,384]{1,0:T(8,128)S(1)}, f32[48,384]{1,0:T(8,128)S(1)}, u32[]{:S(2)}, u32[]{:S(2)}) %collective-permute-start.5) | collective-permute-done | bytes 73760 | tf_op jit(solution)/shard_map/ppermute | solution.py:13
  84.7 0.1 collective-permute-start.6
  84.8 7.7 %collective-permute-done.6 = f32[48,384]{1,0:T(8,128)S(1)} collective-permute-done((f32[48,384]{1,0:T(8,128)S(1)}, f32[48,384]{1,0:T(8,128)S(1)}, u32[]{:S(2)}, u32[]{:S(2)}) %collective-permute-start.6) | collective-permute-done | bytes 73760 | tf_op jit(solution)/shard_map/ppermute | solution.py:13
  92.5 0.1 collective-permute-start.7
  92.6 7.7 %collective-permute-done.7 = f32[48,384]{1,0:T(8,128)S(1)} collective-permute-done((f32[48,384]{1,0:T(8,128)S(1)}, f32[48,384]{1,0:T(8,128)S(1)}, u32[]{:S(2)}, u32[]{:S(2)}) %collective-permute-start.7) | collective-permute-done | bytes 73760 | tf_op jit(solution)/shard_map/ppermute | solution.py:13
  100.3 0.1 collective-permute-start.8
  100.4 7.7 %collective-permute-done.8 = f32[48,384]{1,0:T(8,128)S(1)} collective-permute-done((f32[48,384]{1,0:T(8,128)S(1)}, f32[48,384]{1,0:T(8,128)S(1)}, u32[]{:S(2)}, u32[]{:S(2)}) %collective-permute-start.8) | collective-permute-done | bytes 73760 | tf_op jit(solution)/shard_map/ppermute | solution.py:13
  108.0 0.1 collective-permute-start.9
  108.1 7.7 %collective-permute-done.9 = f32[48,384]{1,0:T(8,128)S(1)} collective-permute-done((f32[48,384]{1,0:T(8,128)S(1)}, f32[48,384]{1,0:T(8,128)S(1)}, u32[]{:S(2)}, u32[]{:S(2)}) %collective-permute-start.9) | collective-permute-done | bytes 73760 | tf_op jit(solution)/shard_map/ppermute | solution.py:13
  115.8 0.1 collective-permute-start.10
  115.9 7.7 %collective-permute-done.10 = f32[48,384]{1,0:T(8,128)S(1)} collective-permute-done((f32[48,384]{1,0:T(8,128)S(1)}, f32[48,384]{1,0:T(8,128)S(1)}, u32[]{:S(2)}, u32[]{:S(2)}) %collective-permute-start.10) | collective-permute-done | bytes 73760 | tf_op jit(solution)/shard_map/ppermute | solution.py:13
  123.6 0.7 select_bitcast_fusion
  (12 shorter events, 0.1 us)
Async XLA Ops:
  0.0 2.0 %copy-start = (f32[1,1,384,384]{3,2,1,0:T(8,128)S(1)}, f32[1,1,384,384]{3,2,1,0:T(8,128)}, u32[]{:S(2)}) copy-start(f32[1,1,384,384]{3,2,1,0:T(8,128)} %param.9) | copy-start | bytes 1769476
  2.0 2.6 %copy-start.1 = (f32[1,1,384,384]{3,2,1,0:T(8,128)S(1)}, f32[1,1,384,384]{3,2,1,0:T(8,128)}, u32[]{:S(2)}) copy-start(f32[1,1,384,384]{3,2,1,0:T(8,128)} %param.10) | copy-start | bytes 1769476
  38.1 7.8 %collective-permute-start = (f32[48,384]{1,0:T(8,128)S(1)}, f32[48,384]{1,0:T(8,128)S(1)}, u32[]{:S(2)}, u32[]{:S(2)}) collective-permute-start(f32[48,384]{1,0:T(8,128)S(1)} %get-tuple-element.29), channel_id=1, source_target_pairs={{0,8},{8,16},{16,24},{24,32},{32,40},{40,48},{48,56},{56,64},{64,7... | collective-permute-start | bytes 221192 | tf_op jit(solution)/shard_map/ppermute | solution.py:13
  45.8 7.8 %collective-permute-start.1 = (f32[48,384]{1,0:T(8,128)S(1)}, f32[48,384]{1,0:T(8,128)S(1)}, u32[]{:S(2)}, u32[]{:S(2)}) collective-permute-start(f32[48,384]{1,0:T(8,128)S(1)} %add.47), channel_id=1, source_target_pairs={{0,8},{8,16},{16,24},{24,32},{32,40},{40,48},{48,56},{56,64},{64,7... | collective-permute-start | bytes 221192 | tf_op jit(solution)/shard_map/ppermute | solution.py:13
  53.6 7.8 %collective-permute-start.2 = (f32[48,384]{1,0:T(8,128)S(1)}, f32[48,384]{1,0:T(8,128)S(1)}, u32[]{:S(2)}, u32[]{:S(2)}) collective-permute-start(f32[48,384]{1,0:T(8,128)S(1)} %add.48), channel_id=1, source_target_pairs={{0,8},{8,16},{16,24},{24,32},{32,40},{40,48},{48,56},{56,64},{64,7... | collective-permute-start | bytes 221192 | tf_op jit(solution)/shard_map/ppermute | solution.py:13
  61.4 7.8 %collective-permute-start.3 = (f32[48,384]{1,0:T(8,128)S(1)}, f32[48,384]{1,0:T(8,128)S(1)}, u32[]{:S(2)}, u32[]{:S(2)}) collective-permute-start(f32[48,384]{1,0:T(8,128)S(1)} %add.49), channel_id=1, source_target_pairs={{0,8},{8,16},{16,24},{24,32},{32,40},{40,48},{48,56},{56,64},{64,7... | collective-permute-start | bytes 221192 | tf_op jit(solution)/shard_map/ppermute | solution.py:13
  69.2 7.8 %collective-permute-start.4 = (f32[48,384]{1,0:T(8,128)S(1)}, f32[48,384]{1,0:T(8,128)S(1)}, u32[]{:S(2)}, u32[]{:S(2)}) collective-permute-start(f32[48,384]{1,0:T(8,128)S(1)} %add.50), channel_id=1, source_target_pairs={{0,8},{8,16},{16,24},{24,32},{32,40},{40,48},{48,56},{56,64},{64,7... | collective-permute-start | bytes 221192 | tf_op jit(solution)/shard_map/ppermute | solution.py:13
  76.9 7.8 %collective-permute-start.5 = (f32[48,384]{1,0:T(8,128)S(1)}, f32[48,384]{1,0:T(8,128)S(1)}, u32[]{:S(2)}, u32[]{:S(2)}) collective-permute-start(f32[48,384]{1,0:T(8,128)S(1)} %add.51), channel_id=1, source_target_pairs={{0,8},{8,16},{16,24},{24,32},{32,40},{40,48},{48,56},{56,64},{64,7... | collective-permute-start | bytes 221192 | tf_op jit(solution)/shard_map/ppermute | solution.py:13
  84.7 7.8 %collective-permute-start.6 = (f32[48,384]{1,0:T(8,128)S(1)}, f32[48,384]{1,0:T(8,128)S(1)}, u32[]{:S(2)}, u32[]{:S(2)}) collective-permute-start(f32[48,384]{1,0:T(8,128)S(1)} %add.52), channel_id=1, source_target_pairs={{0,8},{8,16},{16,24},{24,32},{32,40},{40,48},{48,56},{56,64},{64,7... | collective-permute-start | bytes 221192 | tf_op jit(solution)/shard_map/ppermute | solution.py:13
  92.5 7.8 %collective-permute-start.7 = (f32[48,384]{1,0:T(8,128)S(1)}, f32[48,384]{1,0:T(8,128)S(1)}, u32[]{:S(2)}, u32[]{:S(2)}) collective-permute-start(f32[48,384]{1,0:T(8,128)S(1)} %add.53), channel_id=1, source_target_pairs={{0,8},{8,16},{16,24},{24,32},{32,40},{40,48},{48,56},{56,64},{64,7... | collective-permute-start | bytes 221192 | tf_op jit(solution)/shard_map/ppermute | solution.py:13
  100.3 7.8 %collective-permute-start.8 = (f32[48,384]{1,0:T(8,128)S(1)}, f32[48,384]{1,0:T(8,128)S(1)}, u32[]{:S(2)}, u32[]{:S(2)}) collective-permute-start(f32[48,384]{1,0:T(8,128)S(1)} %add.54), channel_id=1, source_target_pairs={{0,8},{8,16},{16,24},{24,32},{32,40},{40,48},{48,56},{56,64},{64,7... | collective-permute-start | bytes 221192 | tf_op jit(solution)/shard_map/ppermute | solution.py:13
  108.0 7.8 %collective-permute-start.9 = (f32[48,384]{1,0:T(8,128)S(1)}, f32[48,384]{1,0:T(8,128)S(1)}, u32[]{:S(2)}, u32[]{:S(2)}) collective-permute-start(f32[48,384]{1,0:T(8,128)S(1)} %add.55), channel_id=1, source_target_pairs={{0,8},{8,16},{16,24},{24,32},{32,40},{40,48},{48,56},{56,64},{64,7... | collective-permute-start | bytes 221192 | tf_op jit(solution)/shard_map/ppermute | solution.py:13
  115.8 7.8 %collective-permute-start.10 = (f32[48,384]{1,0:T(8,128)S(1)}, f32[48,384]{1,0:T(8,128)S(1)}, u32[]{:S(2)}, u32[]{:S(2)}) collective-permute-start(f32[48,384]{1,0:T(8,128)S(1)} %add.56), channel_id=1, source_target_pairs={{0,8},{8,16},{16,24},{24,32},{32,40},{40,48},{48,56},{56,64},{64,7... | collective-permute-start | bytes 221192 | tf_op jit(solution)/shard_map/ppermute | solution.py:13

commit v2 on v1

v2 whole, which is shorter than its diff:
```python
import functools

import jax
import jax.numpy as jnp
from jax import lax
from jax.experimental import pallas as pl
from jax.experimental.pallas import tpu as pltpu
from jax.sharding import PartitionSpec as P

B = 384
ROWS = 48
PIECES = 8
CHUNKS = 3
STEP = ROWS // CHUNKS
TARGETS = 13
MESH = pl.DeviceIdType.MESH
F32, BF16 = jnp.float32, jnp.bfloat16

SHIFT_TARGETS = ((0, 1, 8, 9), (2, 3, 10, 11), (4, 5, 12), (6, 7))
SHIFT_START = (0, 4, 8, 11)
PLACE = {t: SHIFT_START[s] + i for s, group in enumerate(SHIFT_TARGETS) for i, t in enumerate(group)}


def halves(value):
    high = value.astype(BF16)
    return high, (value - high.astype(F32)).astype(BF16)


def dot3(a, b, contract):
    dims = (contract, ((), ()))
    one = functools.partial(lax.dot_general, dimension_numbers=dims, preferred_element_type=F32)
    return one(a[0], b[0]) + (one(a[0], b[1]) + one(a[1], b[0]))


def kernel(
    left_dims, right_dims, charges, wave_hbm, left_hbm, right_hbm, out,
    wave, left, right, tag_out, tag_in, y_out, y_in, x_out, x_in, z_out, z_in,
    in_sem, tag_ss, tag_rs, y_ss, y_rs, x_ss, x_rs, z_ss, z_rs,
):
    op, term = lax.axis_index("op"), lax.axis_index("term")
    core, x, z_lo = op % 2, (op // 2) % 4, op // 8
    y, z_hi = term % 4, term // 4
    far = (z_hi != core).astype(jnp.int32)

    def device(z_lo_, x_, core_, z_hi_, y_):
        return {"op": (z_lo_ * 4 + x_) * 2 + core_, "term": z_hi_ * 4 + y_}

    def y_peer(slot):
        return device(z_lo, x, (core + slot) % 2, z_hi, (y + 4 - slot // 2) % 4)

    def y_source(slot):
        return device(z_lo, x, (core + slot) % 2, z_hi, (y + slot // 2) % 4)

    loads = [
        pltpu.make_async_copy(wave_hbm, wave, in_sem.at[0]),
        pltpu.make_async_copy(left_hbm, left, in_sem.at[1]),
        pltpu.make_async_copy(right_hbm, right, in_sem.at[2]),
    ]
    for load in loads:
        load.start()

    barrier = pltpu.get_barrier_semaphore()

    def greet(device_id):
        pl.semaphore_signal(barrier, inc=1, device_id=device_id, device_id_type=MESH)

    for slot in range(1, PIECES):
        greet(y_source(slot))
    for shift in range(1, 4):
        greet(device(z_lo, (x + 4 - shift) % 4, core, z_hi, y))
    for ahead in range(3):
        for half in range(2):
            source = device((z_lo + 4 - ahead) % 4, x, z_hi, (z_hi + half) % 2, y)
            if ahead == 0 and half == 0:
                pl.when(far == 1)(functools.partial(greet, source))
            else:
                greet(source)

    tag_out[...] = jnp.full((8, 128), charges[0, 0] + core, jnp.int32)
    tag_in[0] = tag_out[...]

    loads[0].wait()
    live = (lax.broadcasted_iota(jnp.int32, (B, B), 0) < left_dims[0]) & (
        lax.broadcasted_iota(jnp.int32, (B, B), 1) < right_dims[0]
    )
    wave_parts = halves(jnp.where(live, wave[...], 0.0))
    loads[2].wait()
    right_parts = halves(right[...])
    loads[1].wait()

    def contribution(chunk):
        rows = left[:, chunk * STEP : (chunk + 1) * STEP, :].reshape(PIECES * STEP, B)
        product = dot3(halves(rows), wave_parts, ((1,), (0,)))
        result = dot3(halves(product), right_parts, ((1,), (1,)))
        y_out[chunk] = result.reshape(PIECES, STEP, B)

    def y_copy(chunk, slot):
        peer = y_peer(slot)
        piece = (core + slot) % 2 * 4 + (y + 4 - slot // 2) % 4
        return pltpu.make_async_remote_copy(
            src_ref=y_out.at[chunk, piece],
            dst_ref=y_in.at[chunk, slot],
            send_sem=y_ss.at[chunk, slot],
            recv_sem=y_rs.at[chunk, slot],
            device_id=peer,
            device_id_type=MESH,
        )

    def tag_copy(slot):
        return pltpu.make_async_remote_copy(
            src_ref=tag_out,
            dst_ref=tag_in.at[slot],
            send_sem=tag_ss.at[slot],
            recv_sem=tag_rs.at[slot],
            device_id=y_peer(slot),
            device_id_type=MESH,
        )

    def x_copy(chunk, shift):
        size = len(SHIFT_TARGETS[shift])
        return pltpu.make_async_remote_copy(
            src_ref=x_out.at[chunk, pl.ds(SHIFT_START[shift], size)],
            dst_ref=x_in.at[chunk, pl.ds(SHIFT_START[shift] - 4, size)],
            send_sem=x_ss.at[chunk, shift],
            recv_sem=x_rs.at[chunk, shift],
            device_id=device(z_lo, (x + shift) % 4, core, z_hi, y),
            device_id_type=MESH,
        )

    def z_copy(chunk, ahead, other):
        target_core = (core + other) % 2
        return pltpu.make_async_remote_copy(
            src_ref=z_out.at[chunk, ahead, target_core],
            dst_ref=z_in.at[chunk, ahead * 2 + far],
            send_sem=z_ss.at[chunk, ahead * 2 + other],
            recv_sem=z_rs.at[chunk, ahead * 2 + far],
            device_id=device((z_lo + ahead) % 4, x, target_core, core, y),
            device_id_type=MESH,
        )

    def z_arrival(chunk, slot):
        return pltpu.make_async_remote_copy(
            src_ref=z_out.at[chunk, 0, 0],
            dst_ref=z_in.at[chunk, slot],
            send_sem=z_ss.at[chunk, slot],
            recv_sem=z_rs.at[chunk, slot],
            device_id=device(z_lo, x, (core + 1) % 2, z_hi, y),
            device_id_type=MESH,
        )

    y_order = (4, 5, 2, 3, 6, 7, 1)

    for chunk in range(CHUNKS):
        contribution(chunk)
        if chunk == 0:
            pl.semaphore_wait(barrier, 15 + far)
            for slot in y_order:
                tag_copy(slot).start()
        for slot in y_order:
            y_copy(chunk, slot).start()

    for chunk in range(CHUNKS):
        if chunk == 0:
            for slot in range(1, PIECES):
                tag_copy(slot).wait_recv()
        y_in[chunk, 0] = y_out[chunk, core * 4 + y]
        for slot in range(1, PIECES):
            y_copy(chunk, slot).wait_recv()
        tags = [tag_in[slot] for slot in range(PIECES)]
        for row in range(0, STEP, 8):
            for column in range(0, B, 128):
                spot = (slice(row, row + 8), slice(column, column + 128))
                blocks = [y_in[(chunk, slot) + spot] for slot in range(PIECES)]
                for target in range(TARGETS):
                    parts = [jnp.where(t == target, b, 0.0) for t, b in zip(tags, blocks)]
                    while len(parts) > 1:
                        parts = [a + b for a, b in zip(parts[::2], parts[1::2])]
                    x_out[(chunk, PLACE[target]) + spot] = parts[0]
        for shift in (2, 1, 3):
            x_copy(chunk, shift).start()

    for chunk in range(CHUNKS):
        for shift in range(1, 4):
            x_copy(chunk, shift).wait_recv()
        for q in range(2):
            first = [x_in[chunk, SHIFT_START[s] - 4 + q] for s in (1, 2, 3)]
            second = [x_in[chunk, 2 + q], x_in[chunk, 6] if q == 0 else None]
            near = [x >= s for s in (1, 2, 3)]
            sums = [x_out[chunk, q], x_out[chunk, 2 + q], jnp.zeros((STEP, B), F32)]
            for is_near, block in zip(near, first):
                sums[0] += jnp.where(is_near, block, 0.0)
                sums[1] += jnp.where(is_near, 0.0, block)
            for is_near, block in zip(near, second):
                if block is not None:
                    sums[1] += jnp.where(is_near, block, 0.0)
                    sums[2] += jnp.where(is_near, 0.0, block)
            for ahead in range(3):
                z_out[chunk, ahead, q] = sums[ahead]

        for ahead, other in ((0, 0), (0, 1), (1, 0), (1, 1), (2, 0), (2, 1)):
            if ahead == 0 and other == 0:

                @pl.when(far == 1)
                def _():
                    z_copy(chunk, 0, 0).start()

                @pl.when(far == 0)
                def _():
                    z_in[chunk, 0] = z_out[chunk, 0, core]
            else:
                z_copy(chunk, ahead, other).start()

    for chunk in range(CHUNKS):
        for slot in range(6):
            if slot == 0:

                @pl.when(far == 1)
                def _():
                    z_arrival(chunk, 0).wait_recv()
            else:
                z_arrival(chunk, slot).wait_recv()
        blocks = [z_in[chunk, slot] for slot in range(6)]
        total = (blocks[0] + blocks[1]) + (blocks[2] + blocks[3]) + (blocks[4] + blocks[5])
        out[chunk * STEP : (chunk + 1) * STEP, :] = total

    for slot in range(1, PIECES):
        tag_copy(slot).wait_send()
    for chunk in range(CHUNKS):
        for slot in range(1, PIECES):
            y_copy(chunk, slot).wait_send()
        for shift in range(1, 4):
            x_copy(chunk, shift).wait_send()
        for ahead in range(3):
            for other in range(2):
                if ahead == 0 and other == 0:

                    @pl.when(far == 1)
                    def _():
                        z_copy(chunk, 0, 0).wait_send()
                else:
                    z_copy(chunk, ahead, other).wait_send()


def on_device(wavefunction, left_dims, right_dims, left_operators, right_operators, charges):
    smem = pl.BlockSpec(memory_space=pltpu.SMEM)
    hbm = pl.BlockSpec(memory_space=pl.ANY)
    dma = pltpu.SemaphoreType.DMA
    summed = pl.pallas_call(
        kernel,
        out_shape=jax.ShapeDtypeStruct((ROWS, B), F32),
        in_specs=[smem, smem, smem, hbm, hbm, hbm],
        out_specs=pl.BlockSpec(memory_space=pltpu.VMEM),
        scratch_shapes=[
            pltpu.VMEM((B, B), F32),
            pltpu.VMEM((PIECES, ROWS, B), F32),
            pltpu.VMEM((B, B), F32),
            pltpu.VMEM((8, 128), jnp.int32),
            pltpu.VMEM((PIECES, 8, 128), jnp.int32),
            pltpu.VMEM((CHUNKS, PIECES, STEP, B), F32),
            pltpu.VMEM((CHUNKS, PIECES, STEP, B), F32),
            pltpu.VMEM((CHUNKS, TARGETS, STEP, B), F32),
            pltpu.VMEM((CHUNKS, TARGETS - 4, STEP, B), F32),
            pltpu.VMEM((CHUNKS, 3, 2, STEP, B), F32),
            pltpu.VMEM((CHUNKS, 6, STEP, B), F32),
            dma((3,)),
            dma((PIECES,)),
            dma((PIECES,)),
            dma((CHUNKS, PIECES)),
            dma((CHUNKS, PIECES)),
            dma((CHUNKS, 4)),
            dma((CHUNKS, 4)),
            dma((CHUNKS, 6)),
            dma((CHUNKS, 6)),
        ],
        compiler_params=pltpu.CompilerParams(collective_id=0, has_side_effects=True),
        name="sector_scatter",
    )(
        left_dims,
        right_dims,
        charges,
        wavefunction[0],
        left_operators.reshape(PIECES, ROWS, B),
        right_operators[0, 0],
    )
    row_index = lax.axis_index("term") * ROWS + jnp.arange(ROWS)
    live_rows = ((row_index[:, None] < left_dims[0]) & (jnp.arange(B)[None, :] < right_dims[0])).astype(F32)
    return (summed * live_rows)[None]


def solution(mesh):
    in_specs = (
        P("op", None, None),
        P("op"),
        P("op"),
        P("op", "term", None, None),
        P("op", "term", None, None),
        P("op", "term"),
    )
    out_specs = P("op", "term", None)
    return jax.shard_map(
        on_device, mesh=mesh, in_specs=in_specs, out_specs=out_specs, check_vma=False
    )
```

time: 124 us -> 42.2 us (0.34)
  the two profiles are of different devices: /device:TPU:0 before, /device:TPU:1 now
where the time goes in v2:
time: 42.2 us; the launch traced here: 42.1 us
  Pallas kernels  38.5 us (91%)
  between operations  1.97 us (5%)
  other arithmetic  1.61 us (4%)
    pallas_call x1, Pallas kernels, on_device(): pl.pallas_call(kernel, out_shape=jax.ShapeDtypeStruct((ROWS, B), F32), in...  38.5 us
    broadcast_in_dim x1, other arithmetic, on_device(): return (summed * live_rows)[None]  1.59 us

profile of v2, /device:TPU:1, one launch (start us, length us, event | category | flops | bytes accessed | tf_op | source)
XLA Modules:
  0.0 42.1 jit_solution(202322763781343357)
XLA Ops:
  1.9 38.5 %sector_scatter.1 = f32[48,384]{1,0:T(8,128)} custom-call(s32[1]{0:T(128)} %copy.7.left_dims, s32[1]{0:T(128)} %copy.8.right_dims, s32[1,1]{1,0:T(1,128)S(6)} %copy.9.charges, f32[384,384]{1,0:T(8,128)} %bitcast.9, f32[8,48,384]{2,1,0:T(8,128)} %bitcast.10, f32[384,384]{1,0:T(8,128)} %bitcast.11), custom_call_target="tpu_custom_call" | custom-call | tf_op jit(solution)/shard_map/sector_scatter/pallas_call | solution.py:248
  40.5 1.6 %select_bitcast_fusion = f32[1,48,384]{2,1,0:T(8,128)} fusion(f32[48,384]{1,0:T(8,128)} %sector_scatter.1, pred[384]{0:T(512)(128)(4,1)S(1)} %iota_compare_fusion, pred[48]{0:T(512)(128)(4,1)S(1)} %add_compare_fusion), kind=kLoop, calls=%fused_computation | loop fusion | flops 36864 | bytes 147888 | tf_op jit(solution)/shard_map/broadcast_in_dim | solution.py:287
  (2 shorter events, 0.0 us)

commit v3 on v2

--- a/solution.py
+++ b/solution.py
@@ -10,7 +10,7 @@
 B = 384
 ROWS = 48
 PIECES = 8
-CHUNKS = 3
+CHUNKS = 6
 STEP = ROWS // CHUNKS
 TARGETS = 13
 MESH = pl.DeviceIdType.MESH
@@ -221,7 +221,9 @@
                 z_arrival(chunk, slot).wait_recv()
         blocks = [z_in[chunk, slot] for slot in range(6)]
         total = (blocks[0] + blocks[1]) + (blocks[2] + blocks[3]) + (blocks[4] + blocks[5])
-        out[chunk * STEP : (chunk + 1) * STEP, :] = total
+        rows_ = term * ROWS + chunk * STEP + lax.broadcasted_iota(jnp.int32, (STEP, B), 0)
+        cols_ = lax.broadcasted_iota(jnp.int32, (STEP, B), 1)
+        out[chunk * STEP : (chunk + 1) * STEP, :] = jnp.where((rows_ < left_dims[0]) & (cols_ < right_dims[0]), total, 0.0)
 
     for slot in range(1, PIECES):
         tag_copy(slot).wait_send()
@@ -272,19 +274,17 @@
             dma((CHUNKS, 6)),
             dma((CHUNKS, 6)),
         ],
-        compiler_params=pltpu.CompilerParams(collective_id=0, has_side_effects=True),
+        compiler_params=pltpu.CompilerParams(collective_id=0, has_side_effects=True, vmem_limit_bytes=24 << 20),
         name="sector_scatter",
     )(
         left_dims,
         right_dims,
         charges,
-        wavefunction[0],
-        left_operators.reshape(PIECES, ROWS, B),
-        right_operators[0, 0],
+        pltpu.with_memory_space_constraint(wavefunction[0], pltpu.HBM),
+        pltpu.with_memory_space_constraint(left_operators.reshape(PIECES, ROWS, B), pltpu.HBM),
+        pltpu.with_memory_space_constraint(right_operators[0, 0], pltpu.HBM),
     )
-    row_index = lax.axis_index("term") * ROWS + jnp.arange(ROWS)
-    live_rows = ((row_index[:, None] < left_dims[0]) & (jnp.arange(B)[None, :] < right_dims[0])).astype(F32)
-    return (summed * live_rows)[None]
+    return summed[None]
 
 
 def solution(mesh):

time: 42.2 us -> 38.7 us (0.917)
  Pallas kernels: 38.5 us -> 36 us
  other arithmetic: 1.61 us -> 0 us
  local copies, waits for them, and re-layouts: 0 us -> 0.64 us
    pallas_call x1, Pallas kernels: 38.5 us -> 36 us  [on_device(): pl.pallas_call(kernel, out_shape=jax.ShapeDtypeStruct((ROWS, B), F32), in...]
    broadcast_in_dim x1 -> x0, other arithmetic: 1.59 us -> none  [on_device(): return (summed * live_rows)[None]]
    unnamed x0 -> x1, local copies, waits for them, and re-layouts: none -> 0.64 us
where the time goes in v3:
time: 38.7 us; the launch traced here: 38.6 us
  Pallas kernels  36 us (93%)
  between operations  1.95 us (5%)
  local copies, waits for them, and re-layouts  0.64 us (2%)
    pallas_call x1, Pallas kernels, on_device(): pl.pallas_call(kernel, out_shape=jax.ShapeDtypeStruct((ROWS, B), F32), in...  36 us

profile of v3, /device:TPU:1, one launch (start us, length us, event | category | flops | bytes accessed | tf_op | source)
XLA Modules:
  0.0 38.6 jit_solution(8680909627226234481)
XLA Ops:
  1.9 36.0 %sector_scatter.1 = f32[48,384]{1,0:T(8,128)S(1)} custom-call(s32[1]{0:T(128)S(6)} %copy.8.left_dims, s32[1]{0:T(128)S(6)} %copy.9.right_dims, s32[1,1]{1,0:T(1,128)S(6)} %copy.10.charges, f32[384,384]{1,0:T(8,128)} %bitcast.5, f32[8,48,384]{2,1,0:T(8,128)} %bitcast.6, f32[384,384]{1,0:T(8,128)} %bitcast.7), custom_call_target="tpu_custom_call" | custom-call | tf_op jit(solution)/shard_map/sector_scatter/pallas_call | solution.py:250
  38.0 0.6 %copy.11 = f32[1,48,384]{2,1,0:T(8,128)} copy(f32[1,48,384]{2,1,0:T(8,128)S(1)} %bitcast.4) | data formatting | bytes 147456

commit v4 on v1

v4 whole, which is shorter than its diff:
```python
import functools

import jax
import jax.numpy as jnp
from jax import lax
from jax.experimental import pallas as pl
from jax.experimental.pallas import tpu as pltpu
from jax.sharding import PartitionSpec as P

B = 384
ROWS = 48
PIECES = 8
CHUNKS = 3
STEP = ROWS // CHUNKS
SUB = STEP // 4
SOURCES = 32
TARGETS = 19
MESH = pl.DeviceIdType.MESH
F32, BF16 = jnp.float32, jnp.bfloat16


def halves(value):
    high = value.astype(BF16)
    return high, (value - high.astype(F32)).astype(BF16)


def dot3(a, b, contract):
    dims = (contract, ((), ()))
    one = functools.partial(lax.dot_general, dimension_numbers=dims, preferred_element_type=F32)
    return one(a[0], b[0]) + (one(a[0], b[1]) + one(a[1], b[0]))


def kernel(
    left_dims, right_dims, charges, wave_hbm, left_hbm, right_hbm, out,
    wave, left, right, tag_out, tag_in, plane_out, plane_in, deep_out, deep_in,
    in_sem, tag_ss, tag_rs, plane_ss, plane_rs, deep_ss, deep_rs, last_rs,
):
    op, term = lax.axis_index("op"), lax.axis_index("term")
    core, x, z_lo = op % 2, (op // 2) % 4, op // 8
    y, z_hi = term % 4, term // 4
    far = (z_hi + core) % 2
    local = 2 * x + core
    mine = local * 4 + y

    def device(z_lo_, x_, core_, z_hi_, y_):
        return {"op": (z_lo_ * 4 + x_) * 2 + core_, "term": z_hi_ * 4 + y_}

    loads = [
        pltpu.make_async_copy(wave_hbm, wave, in_sem.at[0]),
        pltpu.make_async_copy(left_hbm, left, in_sem.at[1]),
        pltpu.make_async_copy(right_hbm, right, in_sem.at[2]),
    ]
    for load in loads:
        load.start()

    barrier = pltpu.get_barrier_semaphore()

    def greet(device_id):
        pl.semaphore_signal(barrier, inc=1, device_id=device_id, device_id_type=MESH)

    steps = [(dx, dy, dc) for dx in (2, 1, 3, 0) for dy in (2, 1, 3, 0) for dc in (0, 1)][:-2] + [(0, 0, 1)]

    def plane_peer(step):
        dx, dy, dc = step
        return (x + dx) % 4, (y + dy) % 4, (core + dc) % 2

    for ahead, half in ((1, 0), (1, 1), (0, 1)):
        for x_ in range(4):
            greet(device((z_lo + 4 - ahead) % 4, x_, z_hi, (z_hi + half) % 2, y))

    @pl.when(local < TARGETS - 16)
    def _():
        for half in range(2):
            for x_ in range(4):
                greet(device((z_lo + 2) % 4, x_, z_hi, (z_hi + half) % 2, y))

    for step in steps:
        x_, y_, core_ = plane_peer(step)
        greet(device(z_lo, x_, core_, z_hi, y_))

    tag_out[...] = jnp.full((1, 128), charges[0, 0] + local, jnp.int32)
    tag_in[mine] = tag_out[...]

    loads[0].wait()
    live = (lax.broadcasted_iota(jnp.int32, (B, B), 0) < left_dims[0]) & (
        lax.broadcasted_iota(jnp.int32, (B, B), 1) < right_dims[0]
    )
    wave_parts = halves(jnp.where(live, wave[...], 0.0))
    loads[2].wait()
    right_parts = halves(right[...])
    loads[1].wait()

    def contribution(chunk):
        rows = left[:, chunk * STEP : (chunk + 1) * STEP, :].reshape(PIECES * STEP, B)
        product = dot3(halves(rows), wave_parts, ((1,), (0,)))
        result = dot3(halves(product), right_parts, ((1,), (1,)))
        for piece in range(PIECES):
            for place in range(4):
                row = piece * STEP + place * SUB
                plane_out[chunk, piece, place] = result[row : row + SUB]

    def plane_copy(chunk, step):
        x_, y_, core_ = plane_peer(step)
        return pltpu.make_async_remote_copy(
            src_ref=plane_out.at[chunk, core_ * 4 + y_, x_],
            dst_ref=plane_in.at[chunk, mine],
            send_sem=plane_ss.at[chunk],
            recv_sem=plane_rs.at[chunk],
            device_id=device(z_lo, x_, core_, z_hi, y_),
            device_id_type=MESH,
        )

    def tag_copy(step):
        x_, y_, core_ = plane_peer(step)
        return pltpu.make_async_remote_copy(
            src_ref=tag_out,
            dst_ref=tag_in.at[mine],
            send_sem=tag_ss,
            recv_sem=tag_rs,
            device_id=device(z_lo, x_, core_, z_hi, y_),
            device_id_type=MESH,
        )

    def bulk(source, target, send_sem, recv_sem):
        return pltpu.make_async_remote_copy(
            src_ref=source,
            dst_ref=target,
            send_sem=send_sem,
            recv_sem=recv_sem,
            device_id=device(z_lo, x, (core + 1) % 2, z_hi, y),
            device_id_type=MESH,
        )

    def deep_copy(chunk, ahead, x_, core_, recv_sem):
        return pltpu.make_async_remote_copy(
            src_ref=deep_out.at[chunk, ahead * 8 + x_ * 2 + core_],
            dst_ref=deep_in.at[chunk, ahead * 2 + far, x],
            send_sem=deep_ss.at[chunk],
            recv_sem=recv_sem,
            device_id=device((z_lo + ahead) % 4, x_, core_, core, y),
            device_id_type=MESH,
        )

    for chunk in range(CHUNKS):
        contribution(chunk)
        if chunk == 0:
            pl.semaphore_wait(barrier, 42 + 8 * far)
            for step in steps:
                tag_copy(step).start()
        for step in steps:
            plane_copy(chunk, step).start()
        plane_in[chunk, mine] = plane_out[chunk, core * 4 + y, x]

    everyone = pl.ds(0, SOURCES - 1)
    for chunk in range(CHUNKS):
        if chunk == 0:
            bulk(tag_in.at[everyone], tag_in.at[everyone], tag_ss, tag_rs).wait_recv()
        bulk(
            plane_in.at[chunk, everyone], plane_in.at[chunk, everyone], plane_ss.at[chunk], plane_rs.at[chunk]
        ).wait_recv()
        for column in range(0, B, 128):
            columns = slice(column, column + 128)
            sums = [None] * TARGETS
            for source in range(SOURCES):
                tag = jnp.broadcast_to(tag_in[source], (SUB, 128))
                block = plane_in[chunk, source, :, columns]
                for target in range(source // 4, source // 4 + 12):
                    part = jnp.where(tag == target, block, 0.0)
                    sums[target] = part if sums[target] is None else sums[target] + part
            for target in range(TARGETS):
                deep_out[chunk, target, :, columns] = sums[target]

        for ahead in (1, 2, 0):
            if ahead == 2:
                for target in range(TARGETS - 16):
                    deep_copy(chunk, 2, target // 2, target % 2, last_rs.at[chunk]).start()
                continue
            for dx in (2, 1, 3, 0):
                for dc in range(2):
                    x_, core_ = (x + dx) % 4, (core + dc) % 2
                    send = functools.partial(
                        lambda *a: deep_copy(*a).start(), chunk, ahead, x_, core_, deep_rs.at[chunk]
                    )
                    if ahead or dx or dc:
                        send()
                    else:
                        pl.when(far == 1)(send)

                        @pl.when(far == 0)
                        def _():
                            deep_in[chunk, 0, x] = deep_out[chunk, local]

    for chunk in range(CHUNKS):

        @pl.when(far == 1)
        def _():
            both = deep_in.at[chunk, pl.ds(0, 4)]
            bulk(both, both, deep_ss.at[chunk], deep_rs.at[chunk]).wait_recv()

        @pl.when(far == 0)
        def _():
            most = plane_in.at[chunk, pl.ds(0, 15)]
            bulk(most, most, deep_ss.at[chunk], deep_rs.at[chunk]).wait_recv()

        def limited(value, place):
            row = term * ROWS + chunk * STEP + place * SUB + lax.broadcasted_iota(jnp.int32, (SUB, B), 0)
            column = lax.broadcasted_iota(jnp.int32, (SUB, B), 1)
            return jnp.where((row < left_dims[0]) & (column < right_dims[0]), value, 0.0)

        def total(slots, place):
            value = deep_in[chunk, slots[0], place]
            for slot in slots[1:]:
                value += deep_in[chunk, slot, place]
            return value

        def spot(place):
            start = chunk * STEP + place * SUB
            return slice(start, start + SUB)

        @pl.when(local < TARGETS - 16)
        def _():
            rest = deep_in.at[chunk, pl.ds(4, 2)]
            bulk(rest, rest, deep_ss.at[chunk], last_rs.at[chunk]).wait_recv()
            for place in range(4):
                out[spot(place), :] = limited(total(range(6), place), place)

        @pl.when(local >= TARGETS - 16)
        def _():
            for place in range(4):
                out[spot(place), :] = limited(total(range(4), place), place)

    bulk(tag_in.at[everyone], tag_in.at[everyone], tag_ss, tag_rs).wait_send()
    for chunk in range(CHUNKS):
        bulk(
            plane_in.at[chunk, everyone], plane_in.at[chunk, everyone], plane_ss.at[chunk], plane_rs.at[chunk]
        ).wait_send()

        @pl.when(far == 1)
        def _():
            bulk(deep_out.at[chunk], deep_out.at[chunk], deep_ss.at[chunk], deep_rs.at[chunk]).wait_send()

        @pl.when(far == 0)
        def _():
            most = deep_out.at[chunk, pl.ds(0, TARGETS - 1)]
            bulk(most, most, deep_ss.at[chunk], deep_rs.at[chunk]).wait_send()


def on_device(wavefunction, left_dims, right_dims, left_operators, right_operators, charges):
    smem = pl.BlockSpec(memory_space=pltpu.SMEM)
    hbm = pl.BlockSpec(memory_space=pl.ANY)
    dma = pltpu.SemaphoreType.DMA
    summed = pl.pallas_call(
        kernel,
        out_shape=jax.ShapeDtypeStruct((ROWS, B), F32),
        in_specs=[smem, smem, smem, hbm, hbm, hbm],
        out_specs=pl.BlockSpec(memory_space=pltpu.VMEM),
        scratch_shapes=[
            pltpu.VMEM((B, B), F32),
            pltpu.VMEM((PIECES, ROWS, B), F32),
            pltpu.VMEM((B, B), F32),
            pltpu.VMEM((1, 128), jnp.int32),
            pltpu.VMEM((SOURCES, 1, 128), jnp.int32),
            pltpu.VMEM((CHUNKS, PIECES, 4, SUB, B), F32),
            pltpu.VMEM((CHUNKS, SOURCES, SUB, B), F32),
            pltpu.VMEM((CHUNKS, TARGETS, SUB, B), F32),
            pltpu.VMEM((CHUNKS, 6, 4, SUB, B), F32),
            dma((3,)),
            dma(()),
            dma(()),
            dma((CHUNKS,)),
            dma((CHUNKS,)),
            dma((CHUNKS,)),
            dma((CHUNKS,)),
            dma((CHUNKS,)),
        ],
        compiler_params=pltpu.CompilerParams(
            collective_id=0, has_side_effects=True, vmem_limit_bytes=24 << 20
        ),
        name="sector_scatter",
    )(
        left_dims,
        right_dims,
        charges,
        pltpu.with_memory_space_constraint(wavefunction[0], pltpu.HBM),
        pltpu.with_memory_space_constraint(left_operators.reshape(PIECES, ROWS, B), pltpu.HBM),
        pltpu.with_memory_space_constraint(right_operators[0, 0], pltpu.HBM),
    )
    return summed[None]


def solution(mesh):
    in_specs = (
        P("op", None, None),
        P("op"),
        P("op"),
        P("op", "term", None, None),
        P("op", "term", None, None),
        P("op", "term"),
    )
    out_specs = P("op", "term", None)
    return jax.shard_map(
        on_device, mesh=mesh, in_specs=in_specs, out_specs=out_specs, check_vma=False
    )
```

time: 124 us -> 32.6 us (0.26)
  the two profiles are of different devices: /device:TPU:0 before, /device:TPU:33 now
where the time goes in v4:
time: 32.6 us; the launch traced here: 32.5 us
  Pallas kernels  29.9 us (92%)
  between operations  1.95 us (6%)
  local copies, waits for them, and re-layouts  0.64 us (2%)
    pallas_call x1, Pallas kernels, on_device(): pl.pallas_call(kernel, out_shape=jax.ShapeDtypeStruct((ROWS, B), F32), in...  29.9 us

profile of v4, /device:TPU:33, one launch (start us, length us, event | category | flops | bytes accessed | tf_op | source)
XLA Modules:
  0.0 32.5 jit_solution(3858182726660414772)
XLA Ops:
  1.9 29.9 %sector_scatter.1 = f32[48,384]{1,0:T(8,128)S(1)} custom-call(s32[1]{0:T(128)S(6)} %copy.8.left_dims, s32[1]{0:T(128)S(6)} %copy.9.right_dims, s32[1,1]{1,0:T(1,128)S(6)} %copy.10.charges, f32[384,384]{1,0:T(8,128)} %bitcast.5, f32[8,48,384]{2,1,0:T(8,128)} %bitcast.6, f32[384,384]{1,0:T(8,128)} %bitcast.7), custom_call_target="tpu_custom_call" | custom-call | tf_op jit(solution)/shard_map/sector_scatter/pallas_call | solution.py:252
  31.8 0.6 %copy.11 = f32[1,48,384]{2,1,0:T(8,128)} copy(f32[1,48,384]{2,1,0:T(8,128)S(1)} %bitcast.4) | data formatting | bytes 147456

commit v5 on v4

--- a/solution.py
+++ b/solution.py
@@ -10,9 +10,9 @@
 B = 384
 ROWS = 48
 PIECES = 8
-CHUNKS = 3
-STEP = ROWS // CHUNKS
+STEP = 16
 SUB = STEP // 4
+CHUNKS = ((0, 0, 128), (0, 128, 128), (0, 256, 128), (1, 0, 384), (2, 0, 384))
 SOURCES = 32
 TARGETS = 19
 MESH = pl.DeviceIdType.MESH
@@ -45,12 +45,17 @@
     def device(z_lo_, x_, core_, z_hi_, y_):
         return {"op": (z_lo_ * 4 + x_) * 2 + core_, "term": z_hi_ * 4 + y_}
 
-    loads = [
-        pltpu.make_async_copy(wave_hbm, wave, in_sem.at[0]),
-        pltpu.make_async_copy(left_hbm, left, in_sem.at[1]),
-        pltpu.make_async_copy(right_hbm, right, in_sem.at[2]),
-    ]
-    for load in loads:
+    def left_load(block):
+        rows = pl.ds(block * STEP, STEP)
+        return pltpu.make_async_copy(left_hbm.at[:, rows], left.at[:, rows], in_sem.at[1 + block])
+
+    def right_load(chunk):
+        rows = pl.ds(CHUNKS[chunk][1], CHUNKS[chunk][2])
+        return pltpu.make_async_copy(right_hbm.at[rows], right.at[rows], in_sem.at[4 + chunk])
+
+    wave_load = pltpu.make_async_copy(wave_hbm, wave, in_sem.at[0])
+    right_loads = [right_load(chunk) for chunk in range(len(CHUNKS)) if CHUNKS[chunk][0] == 0]
+    for load in (wave_load, left_load(0), *right_loads, left_load(1), left_load(2)):
         load.start()
 
     barrier = pltpu.get_barrier_semaphore()
@@ -81,29 +86,36 @@
     tag_out[...] = jnp.full((1, 128), charges[0, 0] + local, jnp.int32)
     tag_in[mine] = tag_out[...]
 
-    loads[0].wait()
+    wave_load.wait()
     live = (lax.broadcasted_iota(jnp.int32, (B, B), 0) < left_dims[0]) & (
         lax.broadcasted_iota(jnp.int32, (B, B), 1) < right_dims[0]
     )
     wave_parts = halves(jnp.where(live, wave[...], 0.0))
-    loads[2].wait()
-    right_parts = halves(right[...])
-    loads[1].wait()
+    products, right_parts = {}, {}
 
     def contribution(chunk):
-        rows = left[:, chunk * STEP : (chunk + 1) * STEP, :].reshape(PIECES * STEP, B)
-        product = dot3(halves(rows), wave_parts, ((1,), (0,)))
-        result = dot3(halves(product), right_parts, ((1,), (1,)))
-        for piece in range(PIECES):
-            for place in range(4):
-                row = piece * STEP + place * SUB
-                plane_out[chunk, piece, place] = result[row : row + SUB]
+        block, start, width = CHUNKS[chunk]
+        if block not in products:
+            left_load(block).wait()
+            rows = left[:, block * STEP : (block + 1) * STEP, :].reshape(PIECES * STEP, B)
+            products[block] = halves(dot3(halves(rows), wave_parts, ((1,), (0,))))
+        if block == 0:
+            right_load(chunk).wait()
+            right_parts[start] = halves(right[start : start + width])
+        for first, part in right_parts.items():
+            if start <= first < start + width:
+                result = dot3(products[block], part, ((1,), (1,)))
+                columns = slice(first - start, first - start + part[0].shape[0])
+                for piece in range(PIECES):
+                    for place in range(4):
+                        row = piece * STEP + place * SUB
+                        plane_out[chunk][piece, place, :, columns] = result[row : row + SUB]
 
     def plane_copy(chunk, step):
         x_, y_, core_ = plane_peer(step)
         return pltpu.make_async_remote_copy(
-            src_ref=plane_out.at[chunk, core_ * 4 + y_, x_],
-            dst_ref=plane_in.at[chunk, mine],
+            src_ref=plane_out[chunk].at[core_ * 4 + y_, x_],
+            dst_ref=plane_in[chunk].at[mine],
             send_sem=plane_ss.at[chunk],
             recv_sem=plane_rs.at[chunk],
             device_id=device(z_lo, x_, core_, z_hi, y_),
@@ -133,15 +145,15 @@
 
     def deep_copy(chunk, ahead, x_, core_, recv_sem):
         return pltpu.make_async_remote_copy(
-            src_ref=deep_out.at[chunk, ahead * 8 + x_ * 2 + core_],
-            dst_ref=deep_in.at[chunk, ahead * 2 + far, x],
+            src_ref=deep_out[chunk].at[ahead * 8 + x_ * 2 + core_],
+            dst_ref=deep_in[chunk].at[ahead * 2 + far, x],
             send_sem=deep_ss.at[chunk],
             recv_sem=recv_sem,
             device_id=device((z_lo + ahead) % 4, x_, core_, core, y),
             device_id_type=MESH,
         )
 
-    for chunk in range(CHUNKS):
+    for chunk in range(len(CHUNKS)):
         contribution(chunk)
         if chunk == 0:
             pl.semaphore_wait(barrier, 42 + 8 * far)
@@ -149,26 +161,26 @@
                 tag_copy(step).start()
         for step in steps:
             plane_copy(chunk, step).start()
-        plane_in[chunk, mine] = plane_out[chunk, core * 4 + y, x]
+        plane_in[chunk][mine] = plane_out[chunk][core * 4 + y, x]
 
     everyone = pl.ds(0, SOURCES - 1)
-    for chunk in range(CHUNKS):
+    for chunk in range(len(CHUNKS)):
         if chunk == 0:
             bulk(tag_in.at[everyone], tag_in.at[everyone], tag_ss, tag_rs).wait_recv()
         bulk(
-            plane_in.at[chunk, everyone], plane_in.at[chunk, everyone], plane_ss.at[chunk], plane_rs.at[chunk]
+            plane_in[chunk].at[everyone], plane_in[chunk].at[everyone], plane_ss.at[chunk], plane_rs.at[chunk]
         ).wait_recv()
-        for column in range(0, B, 128):
+        for column in range(0, CHUNKS[chunk][2], 128):
             columns = slice(column, column + 128)
             sums = [None] * TARGETS
             for source in range(SOURCES):
                 tag = jnp.broadcast_to(tag_in[source], (SUB, 128))
-                block = plane_in[chunk, source, :, columns]
+                block = plane_in[chunk][source, :, columns]
                 for target in range(source // 4, source // 4 + 12):
                     part = jnp.where(tag == target, block, 0.0)
                     sums[target] = part if sums[target] is None else sums[target] + part
             for target in range(TARGETS):
-                deep_out[chunk, target, :, columns] = sums[target]
+                deep_out[chunk][target, :, columns] = sums[target]
 
         for ahead in (1, 2, 0):
             if ahead == 2:
@@ -188,60 +200,62 @@
 
                         @pl.when(far == 0)
                         def _():
-                            deep_in[chunk, 0, x] = deep_out[chunk, local]
-
-    for chunk in range(CHUNKS):
+                            deep_in[chunk][0, x] = deep_out[chunk][local]
+
+    for chunk in range(len(CHUNKS)):
 
         @pl.when(far == 1)
         def _():
-            both = deep_in.at[chunk, pl.ds(0, 4)]
+            both = deep_in[chunk].at[pl.ds(0, 4)]
             bulk(both, both, deep_ss.at[chunk], deep_rs.at[chunk]).wait_recv()
 
         @pl.when(far == 0)
         def _():
-            most = plane_in.at[chunk, pl.ds(0, 15)]
+            most = plane_in[chunk].at[pl.ds(0, 15)]
             bulk(most, most, deep_ss.at[chunk], deep_rs.at[chunk]).wait_recv()
 
+        block, start, width = CHUNKS[chunk]
+
         def limited(value, place):
-            row = term * ROWS + chunk * STEP + place * SUB + lax.broadcasted_iota(jnp.int32, (SUB, B), 0)
-            column = lax.broadcasted_iota(jnp.int32, (SUB, B), 1)
+            row = term * ROWS + block * STEP + place * SUB + lax.broadcasted_iota(jnp.int32, (SUB, width), 0)
+            column = start + lax.broadcasted_iota(jnp.int32, (SUB, width), 1)
             return jnp.where((row < left_dims[0]) & (column < right_dims[0]), value, 0.0)
 
         def total(slots, place):
-            value = deep_in[chunk, slots[0], place]
+            value = deep_in[chunk][slots[0], place]
             for slot in slots[1:]:
-                value += deep_in[chunk, slot, place]
+                value += deep_in[chunk][slot, place]
             return value
 
         def spot(place):
-            start = chunk * STEP + place * SUB
-            return slice(start, start + SUB)
+            row = block * STEP + place * SUB
+            return slice(row, row + SUB), slice(start, start + width)
 
         @pl.when(local < TARGETS - 16)
         def _():
-            rest = deep_in.at[chunk, pl.ds(4, 2)]
+            rest = deep_in[chunk].at[pl.ds(4, 2)]
             bulk(rest, rest, deep_ss.at[chunk], last_rs.at[chunk]).wait_recv()
             for place in range(4):
-                out[spot(place), :] = limited(total(range(6), place), place)
+                out[spot(place)] = limited(total(range(6), place), place)
 
         @pl.when(local >= TARGETS - 16)
         def _():
             for place in range(4):
-                out[spot(place), :] = limited(total(range(4), place), place)
+                out[spot(place)] = limited(total(range(4), place), place)
 
     bulk(tag_in.at[everyone], tag_in.at[everyone], tag_ss, tag_rs).wait_send()
-    for chunk in range(CHUNKS):
+    for chunk in range(len(CHUNKS)):
         bulk(
-            plane_in.at[chunk, everyone], plane_in.at[chunk, everyone], plane_ss.at[chunk], plane_rs.at[chunk]
+            plane_in[chunk].at[everyone], plane_in[chunk].at[everyone], plane_ss.at[chunk], plane_rs.at[chunk]
         ).wait_send()
 
         @pl.when(far == 1)
         def _():
-            bulk(deep_out.at[chunk], deep_out.at[chunk], deep_ss.at[chunk], deep_rs.at[chunk]).wait_send()
+            bulk(deep_out[chunk], deep_out[chunk], deep_ss.at[chunk], deep_rs.at[chunk]).wait_send()
 
         @pl.when(far == 0)
         def _():
-            most = deep_out.at[chunk, pl.ds(0, TARGETS - 1)]
+            most = deep_out[chunk].at[pl.ds(0, TARGETS - 1)]
             bulk(most, most, deep_ss.at[chunk], deep_rs.at[chunk]).wait_send()
 
 
@@ -249,6 +263,10 @@
     smem = pl.BlockSpec(memory_space=pltpu.SMEM)
     hbm = pl.BlockSpec(memory_space=pl.ANY)
     dma = pltpu.SemaphoreType.DMA
+
+    def per_chunk(*leading):
+        return [pltpu.VMEM((*leading, SUB, width), F32) for _, _, width in CHUNKS]
+
     summed = pl.pallas_call(
         kernel,
         out_shape=jax.ShapeDtypeStruct((ROWS, B), F32),
@@ -260,18 +278,18 @@
             pltpu.VMEM((B, B), F32),
             pltpu.VMEM((1, 128), jnp.int32),
             pltpu.VMEM((SOURCES, 1, 128), jnp.int32),
-            pltpu.VMEM((CHUNKS, PIECES, 4, SUB, B), F32),
-            pltpu.VMEM((CHUNKS, SOURCES, SUB, B), F32),
-            pltpu.VMEM((CHUNKS, TARGETS, SUB, B), F32),
-            pltpu.VMEM((CHUNKS, 6, 4, SUB, B), F32),
-            dma((3,)),
+            per_chunk(PIECES, 4),
+            per_chunk(SOURCES),
+            per_chunk(TARGETS),
+            per_chunk(6, 4),
+            dma((4 + len(CHUNKS),)),
             dma(()),
             dma(()),
-            dma((CHUNKS,)),
-            dma((CHUNKS,)),
-            dma((CHUNKS,)),
-            dma((CHUNKS,)),
-            dma((CHUNKS,)),
+            dma((len(CHUNKS),)),
+            dma((len(CHUNKS),)),
+            dma((len(CHUNKS),)),
+            dma((len(CHUNKS),)),
+            dma((len(CHUNKS),)),
         ],
         compiler_params=pltpu.CompilerParams(
             collective_id=0, has_side_effects=True, vmem_limit_bytes=24 << 20

time: 32.6 us -> 31.6 us (0.969)
  the two profiles are of different devices: /device:TPU:33 before, /device:TPU:1 now
where the time goes in v5:
time: 31.6 us; the launch traced here: 31.5 us
  Pallas kernels  28.9 us (91%)
  between operations  1.95 us (6%)
  local copies, waits for them, and re-layouts  0.64 us (2%)
    pallas_call x1, Pallas kernels, on_device(): pl.pallas_call(kernel, out_shape=jax.ShapeDtypeStruct((ROWS, B), F32), in...  28.9 us
    unnamed x1, local copies, waits for them, and re-layouts  0.64 us

profile of v5, /device:TPU:1, one launch (start us, length us, event | category | flops | bytes accessed | tf_op | source)
XLA Modules:
  0.0 31.5 jit_solution(8240233401863292188)
XLA Ops:
  1.9 28.9 %sector_scatter.1 = f32[48,384]{1,0:T(8,128)S(1)} custom-call(s32[1]{0:T(128)S(6)} %copy.8.left_dims, s32[1]{0:T(128)S(6)} %copy.9.right_dims, s32[1,1]{1,0:T(1,128)S(6)} %copy.10.charges, f32[384,384]{1,0:T(8,128)} %bitcast.5, f32[8,48,384]{2,1,0:T(8,128)} %bitcast.6, f32[384,384]{1,0:T(8,128)} %bitcast.7), custom_call_target="tpu_custom_call" | custom-call | tf_op jit(solution)/shard_map/sector_scatter/pallas_call | solution.py:270
  30.8 0.6 %copy.11 = f32[1,48,384]{2,1,0:T(8,128)} copy(f32[1,48,384]{2,1,0:T(8,128)S(1)} %bitcast.4) | data formatting | bytes 147456

commit v6 on v5

--- a/solution.py
+++ b/solution.py
@@ -63,11 +63,14 @@
     def greet(device_id):
         pl.semaphore_signal(barrier, inc=1, device_id=device_id, device_id_type=MESH)
 
-    steps = [(dx, dy, dc) for dx in (2, 1, 3, 0) for dy in (2, 1, 3, 0) for dc in (0, 1)][:-2] + [(0, 0, 1)]
+    places = [(dx, dy) for dx in (2, 1, 3, 0) for dy in (2, 1, 3, 0)][:-1]
+    to_first, to_second = ([(dx, dy, core_) for dx, dy in places] for core_ in range(2))
+    beside = [(0, 0, (core + 1) % 2)]
+    steps = [*to_first, *to_second, *beside]
 
     def plane_peer(step):
-        dx, dy, dc = step
-        return (x + dx) % 4, (y + dy) % 4, (core + dc) % 2
+        dx, dy, core_ = step
+        return (x + dx) % 4, (y + dy) % 4, core_
 
     for ahead, half in ((1, 0), (1, 1), (0, 1)):
         for x_ in range(4):
@@ -159,9 +162,16 @@
             pl.semaphore_wait(barrier, 42 + 8 * far)
             for step in steps:
                 tag_copy(step).start()
-        for step in steps:
+        for step in (*to_first, *beside):
             plane_copy(chunk, step).start()
+        if chunk > 1:
+            for step in to_second:
+                plane_copy(chunk - 2, step).start()
         plane_in[chunk][mine] = plane_out[chunk][core * 4 + y, x]
+
+    for chunk in range(len(CHUNKS) - 2, len(CHUNKS)):
+        for step in to_second:
+            plane_copy(chunk, step).start()
 
     everyone = pl.ds(0, SOURCES - 1)
     for chunk in range(len(CHUNKS)):

time: 31.6 us -> 31.2 us (0.987)
  Pallas kernels: 28.9 us -> 28.5 us
    pallas_call x1, Pallas kernels: 28.9 us -> 28.5 us  [on_device(): pl.pallas_call(kernel, out_shape=jax.ShapeDtypeStruct((ROWS, B), F32), in...]
where the time goes in v6:
time: 31.2 us; the launch traced here: 31.1 us
  Pallas kernels  28.5 us (91%)
  between operations  1.95 us (6%)
  local copies, waits for them, and re-layouts  0.64 us (2%)
    pallas_call x1, Pallas kernels, on_device(): pl.pallas_call(kernel, out_shape=jax.ShapeDtypeStruct((ROWS, B), F32), in...  28.5 us
    unnamed x1, local copies, waits for them, and re-layouts  0.64 us

profile of v6, /device:TPU:1, one launch (start us, length us, event | category | flops | bytes accessed | tf_op | source)
XLA Modules:
  0.0 31.1 jit_solution(17766604279597389421)
XLA Ops:
  1.9 28.5 %sector_scatter.1 = f32[48,384]{1,0:T(8,128)S(1)} custom-call(s32[1]{0:T(128)S(6)} %copy.8.left_dims, s32[1]{0:T(128)S(6)} %copy.9.right_dims, s32[1,1]{1,0:T(1,128)S(6)} %copy.10.charges, f32[384,384]{1,0:T(8,128)} %bitcast.5, f32[8,48,384]{2,1,0:T(8,128)} %bitcast.6, f32[384,384]{1,0:T(8,128)} %bitcast.7), custom_call_target="tpu_custom_call" | custom-call | tf_op jit(solution)/shard_map/sector_scatter/pallas_call | solution.py:280
  30.4 0.6 %copy.11 = f32[1,48,384]{2,1,0:T(8,128)} copy(f32[1,48,384]{2,1,0:T(8,128)S(1)} %bitcast.4) | data formatting | bytes 147456
